TPU v7x, 32 devices: a whole 2x2x4 slice. The times are simulated.
32 devices in a mesh: loop: 16 (over z, y, core), narrow: 2 (over x).
Axes of the slice: x: 2, y: 2, z: 4, core: 2. Of those that a mesh axis runs over, the one named last changes fastest.
Arguments:
- queries: bfloat16 [8192, 4096], P(('loop', 'narrow')), may hold values from -2 to 2
- passages: bfloat16 [64, 4096], P('loop'), may hold values from -10 to 10
- pos_ids: int32 [8192], P(('loop', 'narrow')), may hold values from 0 to 63
- neg_ids: int32 [8192, 32], P(('loop', 'narrow')), may hold values from 0 to 63
- neg_mask: int32 [8192, 32], P(('loop', 'narrow')), may hold values 0 or 1
- neg_counts: int32 [8192], P(('loop', 'narrow')), may hold values from 0 to 32
- d_loss: float32 [8192], P(('loop', 'narrow')), may hold values from -6 to 6
Outputs:
- query_loss: float32 [8192], P(('loop', 'narrow'))
- grad_queries: bfloat16 [8192, 4096], P(('loop', 'narrow'))
- grad_passages: bfloat16 [64, 4096], P('loop')
Inputs may be any that keep to these rules, and one draw needn't show every extreme that they name: `neg_counts`: slots at or beyond a query's count are padding.
All inputs are finite; a program needn't handle non-finite values. No bound on the sum of `neg_mask` on one device may be relied on, other than what follows from the above.
Results may differ from a plain program's by a relative error of at most 0.0058.
Values may be sent and summed in bfloat16 or wider, within the bound.
No kernel may reach another device: no remote copies, remote signals or barrier semaphores. Data moves between devices by JAX's collectives and lax.ppermute only.
A program may use at most 64 MiB of HBM per device.

v0:
```python
import jax
import jax.numpy as jnp
from jax import lax
from jax.sharding import PartitionSpec as P

NEG = 32
logit_scale = 50.0
norm_eps = 1e-06


def normalize(rows):
    wide = rows.astype(jnp.float32)
    scales = lax.rsqrt(jnp.sum(wide * wide, axis=-1) + norm_eps)
    return (scales, (wide * scales[:, None]).astype(jnp.bfloat16))


def weight_table(valid, neg_ids, pool_size):
    columns = jnp.arange(pool_size, dtype=jnp.int32)
    weights = jnp.ones((neg_ids.shape[0], pool_size), jnp.float32)
    for first in range(0, NEG, 8):
        named = neg_ids[:, first : first + 8]
        usable = valid[:, first : first + 8]
        hits = (named[:, :, None] == columns[None, None, :]) & usable[:, :, None]
        weights = weights + jnp.sum(hits.astype(jnp.float32), axis=1)
    return weights


def tangent_back(rows, scales, direction):
    unit = rows.astype(jnp.float32) * scales[:, None]
    inner = jnp.sum(unit * direction, axis=-1, keepdims=True)
    return (scales[:, None] * (direction - unit * inner)).astype(jnp.bfloat16)


def local(queries, passages, pos_ids, neg_ids, neg_mask, neg_counts, d_loss):
    qscale, qnorm = normalize(queries)
    pscale, pnorm = normalize(passages)
    pool = lax.all_gather(pnorm, "loop", axis=0, tiled=True)
    pool_size = pool.shape[0]
    columns = jnp.arange(pool_size, dtype=jnp.int32)
    slots = jnp.arange(NEG, dtype=jnp.int32)
    scores = logit_scale * lax.dot_general(
        qnorm, pool, (((1,), (1,)), ((), ())), preferred_element_type=jnp.float32
    )
    valid = (neg_mask == 1) & (slots[None, :] < neg_counts[:, None])
    weights = weight_table(valid, neg_ids, pool_size)
    terms = weights * jnp.exp(scores)
    denom = jnp.sum(terms, axis=1)
    chosen = columns[None, :] == pos_ids[:, None]
    picked = jnp.sum(jnp.where(chosen, scores, 0.0), axis=1)
    query_loss = jnp.log(denom) - picked
    coef = (
        logit_scale * d_loss[:, None] * (terms / denom[:, None] - chosen.astype(jnp.float32))
    ).astype(jnp.bfloat16)
    qdir = jnp.dot(coef, pool, preferred_element_type=jnp.float32)
    grad_queries = tangent_back(queries, qscale, qdir)
    partial_dir = lax.psum_scatter(
        lax.dot_general(coef, qnorm, (((0,), (0,)), ((), ())), preferred_element_type=jnp.float32),
        "loop",
        scatter_dimension=0,
        tiled=True,
    )
    pdir = lax.psum(partial_dir, "narrow")
    grad_passages = tangent_back(passages, pscale, pdir)
    return (query_loss, grad_queries, grad_passages)


def solution(mesh):
    return jax.shard_map(
        local,
        mesh=mesh,
        in_specs=(
            P(("loop", "narrow"), None),
            P("loop", None),
            P(("loop", "narrow")),
            P(("loop", "narrow"), None),
            P(("loop", "narrow"), None),
            P(("loop", "narrow")),
            P(("loop", "narrow")),
        ),
        out_specs=(P(("loop", "narrow")), P(("loop", "narrow"), None), P("loop", None)),
        check_vma=False,
    )
```

profile of v0, /device:TPU:0, one launch (start us, length us, event | category | flops | bytes accessed | tf_op | source)
XLA Modules:
  0.0 164.1 jit_solution(8291174964269630213)
XLA Ops:
  7.2 0.0 copy-start
  7.2 0.0 copy-start.2
  7.2 0.0 all-reduce.6.cloned.1.call-start
  7.2 1.0 fusion.22
  8.3 2.1 %fusion.7 = f32[256]{0:T(256)S(1)} fusion(bf16[256,4096]{1,0:T(8,128)(2,1)} %param.7), kind=kLoop, calls=%fused_computation.9 | loop fusion | flops 3145472 | bytes 2098176 | tf_op jit(solution)/shard_map/reduce_sum | solution.py:13
  10.4 0.8 fusion.24
  11.2 0.8 fusion.23
  12.0 0.8 fusion.27
  12.8 24.6 %all-gather = bf16[16,4,4096]{2,1,0:T(4,128)(2,1)S(1)} all-gather(bf16[1,4,4096]{2,1,0:T(4,128)(2,1)S(1)} %fusion.23), channel_id=1, replica_groups=mesh['loop'=16,'narrow'=2] {'loop'}, dimensions={0}, use_global_device_ids=true | all-gather | bytes 557056 | tf_op jit(solution)/shard_map/all_gather | solution.py:37
  37.4 0.1 reshape.30
  37.5 0.7 add_rsqrt_fusion
  38.2 0.2 convert_reduce_fusion.2
  38.4 0.2 convert_reduce_fusion
  38.6 0.0 copy-done
  38.6 0.0 copy-done.2
  38.6 0.9 fusion.26
  39.4 1.7 %fusion.8 = f32[64,4096]{1,0:T(8,128)} fusion(bf16[256,4096]{1,0:T(8,128)(2,1)S(1)} %copy-done, f32[256]{0:T(256)S(1)} %get-tuple-element.20, f32[256,64]{0,1:T(8,128)S(1)} %get-tuple-element.4, f32[256]{0:T(256)S(1)} %get-tuple-element.3, f32[256]{0:T(256)S(1)} %get-tuple-element.21, s32[256]{0:T(256)S(1)} %copy-done.2), kind=kOutput, calls=%fused_computation.11 | convolution fusion | flops 137461760 | bytes 3215360 | tf_op jit(solution)/shard_map/dot_general | solution.py:57
  41.1 0.0 all-reduce.6.cloned.1.call-update
  41.1 0.0 all-reduce.4.cloned.1.call-start
  41.2 0.9 fusion.3
  42.1 0.0 copy-start.1
  42.1 2.5 %fusion.6 = bf16[256,4096]{1,0:T(8,128)(2,1)} fusion(f32[256,4096]{1,0:T(8,128)S(1)} %get-tuple-element.15, bf16[256,4096]{1,0:T(8,128)(2,1)S(1)} %copy-done, f32[256]{0:T(256)S(1)} %get-tuple-element.14, f32[256]{0:T(256)S(1)} %get-tuple-element.20), kind=kLoop, calls=%fused_computation.8 | loop fusion | flops 6291456 | bytes 8390656 | tf_op jit(solution)/shard_map/convert_element_type | solution.py:31
  44.6 0.0 copy-done.3
  44.6 0.6 dynamic-slice
  45.8 86.6 %all-reduce.6.cloned.1.call-done = f32[64,4096]{1,0:T(8,128)} async-done(((f32[64,4096]{1,0:T(8,128)}), f32[64,4096]{1,0:T(8,128)}) %all-reduce.6.cloned.1.call-update) | async-done | bytes 1048592
  132.4 1.5 constant_dynamic-slice_fusion
  133.9 0.0 all-reduce.4.cloned.1.call-update
  133.9 0.6 log_subtract_fusion
  134.5 20.2 %all-reduce.4.cloned.1.call-done = f32[4,4096]{1,0:T(4,128)} async-done(((f32[4,4096]{1,0:T(4,128)}), f32[4,4096]{1,0:T(4,128)}) %all-reduce.4.cloned.1.call-update) | async-done | bytes 65552 | tf_op jit(solution)/shard_map/psum | solution.py:62
  154.7 0.0 copy-done.1
  154.7 1.1 fusion.18
  155.7 1.5 fusion.21
  (3 shorter events, 0.0 us)
Async XLA Ops:
  7.2 31.4 %copy-start = (bf16[256,4096]{1,0:T(8,128)(2,1)S(1)}, bf16[256,4096]{1,0:T(8,128)(2,1)}, u32[]{:S(2)}) copy-start(bf16[256,4096]{1,0:T(8,128)(2,1)} %param.7) | copy-start | bytes 6291460
  7.2 31.4 %copy-start.2 = (s32[256]{0:T(256)S(1)}, s32[256]{0:T(256)}, u32[]{:S(2)}) copy-start(s32[256]{0:T(256)} %param.9) | copy-start | bytes 3076
  7.2 125.2 %all-reduce.6.cloned.1.call-start = ((), (), s32[]{:S(2)}) async-start(), calls=%async_computation.1 | async-start | bytes 2097152
  41.1 113.5 %all-reduce.4.cloned.1.call-start = ((), (), s32[]{:S(2)}) async-start(), calls=%async_computation | async-start | bytes 131072 | tf_op jit(solution)/shard_map/psum | solution.py:62
  42.1 2.5 %copy-start.3 = (u32[32]{0:T(128)S(1)}, u32[32]{0:T(128)}, u32[]{:S(2)}) copy-start(u32[32]{0:T(128)} %constant.15) | copy-start | bytes 388
  42.1 112.6 %copy-start.1 = (bf16[4,4096]{1,0:T(4,128)(2,1)S(1)}, bf16[4,4096]{1,0:T(4,128)(2,1)}, u32[]{:S(2)}) copy-start(bf16[4,4096]{1,0:T(4,128)(2,1)} %param.8) | copy-start | bytes 98308
Sparse Core Ops, SparseCore 0:
  41.3 91.0 all-reduce.5
  134.6 20.0 all-reduce.3
where the time goes:
time: 165 us; the launch traced here: 164 us
  waiting for transfers between devices  107 us (65%)
  blocking collectives  24.6 us (15%)
  between operations  14.8 us (9%)
  other arithmetic  11.5 us (7%)
  matrix products  3.43 us (2%)
  local copies, waits for them, and re-layouts  3.01 us (2%)
    unnamed x3, waiting for transfers between devices  86.6 us
    all_gather x1, blocking collectives, local(): pool = lax.all_gather(pnorm, 'loop', axis=0, tiled=True)  24.6 us
    psum x1, waiting for transfers between devices, local(): pdir = lax.psum(partial_dir, 'narrow')  20.2 us
    convert_element_type x2, other arithmetic, tangent_back(): return (scales[:, None] * (direction - unit * inner)).astype(jnp.bfloat16)  4.01 us
  transfers between devices with their start and end apart: 2, of which 2 were waited for; matrix products, arithmetic and copies ran while one was open for 3% of the time, Pallas kernels for 0%

commit v1 on v0

--- a/solution.py
+++ b/solution.py
@@ -59,7 +59,7 @@
         scatter_dimension=0,
         tiled=True,
     )
-    pdir = lax.psum(partial_dir, "narrow")
+    pdir = jnp.sum(lax.all_gather(partial_dir, "narrow"), axis=0)
     grad_passages = tangent_back(passages, pscale, pdir)
     return (query_loss, grad_queries, grad_passages)
 

time: 165 us -> 146 us (0.88)
  waiting for transfers between devices: 107 us -> 86 us
  blocking collectives: 24.6 us -> 29.5 us
  other arithmetic: 11.5 us -> 9.83 us
    psum x1 -> x0, waiting for transfers between devices: 20.2 us -> none  [local(): pdir = lax.psum(partial_dir, 'narrow')]
    all_gather x0 -> x1, blocking collectives: none -> 4.93 us  [local(): pdir = jnp.sum(lax.all_gather(partial_dir, 'narrow'), axis=0)]
    unnamed x3 -> x2, waiting for transfers between devices: 86.6 us -> 86 us
  transfers between devices with their start and end apart: 2 -> 1, of which waited for: 2 -> 1; matrix products, arithmetic and copies ran while one was open for 3% -> 3% of each run, Pallas kernels for 0% -> 0%
where the time goes in v1:
time: 146 us
  waiting for transfers between devices  86 us (59%)
  blocking collectives  29.5 us (20%)
  between operations  14.8 us (10%)
  other arithmetic  9.83 us (7%)
  matrix products  3.47 us (2%)
  local copies, waits for them, and re-layouts  2.4 us (2%)
    unnamed x2, waiting for transfers between devices  86 us
    all_gather x1, blocking collectives, local(): pool = lax.all_gather(pnorm, 'loop', axis=0, tiled=True)  24.6 us
    all_gather x1, blocking collectives, local(): pdir = jnp.sum(lax.all_gather(partial_dir, 'narrow'), axis=0)  4.93 us
    convert_element_type x2, other arithmetic, tangent_back(): return (scales[:, None] * (direction - unit * inner)).astype(jnp.bfloat16)  3.18 us
    reduce_sum x2, other arithmetic, normalize(): scales = lax.rsqrt(jnp.sum(wide * wide, axis=-1) + norm_eps)  3.13 us
  transfers between devices with their start and end apart: 1, of which 1 were waited for; matrix products, arithmetic and copies ran while one was open for 3% of the time, Pallas kernels for 0%

profile of v1, /device:TPU:0, one launch (start us, length us, event | category | flops | bytes accessed | tf_op | source)
XLA Modules:
  0.0 146.1 jit_solution(2441135998431496281)
XLA Ops:
  7.2 0.0 copy-start
  7.2 0.0 copy-start.2
  7.2 0.0 all-reduce.3.cloned.1.call-start
  7.2 1.0 fusion.22
  8.3 2.1 %fusion.7 = f32[256]{0:T(256)S(1)} fusion(bf16[256,4096]{1,0:T(8,128)(2,1)} %param.7), kind=kLoop, calls=%fused_computation.9 | loop fusion | flops 3145472 | bytes 2098176 | tf_op jit(solution)/shard_map/reduce_sum | solution.py:13
  10.4 0.8 fusion.24
  11.2 0.8 fusion.23
  12.0 0.8 fusion.27
  12.8 24.6 %all-gather.1 = bf16[16,4,4096]{2,1,0:T(4,128)(2,1)S(1)} all-gather(bf16[1,4,4096]{2,1,0:T(4,128)(2,1)S(1)} %fusion.23), channel_id=1, replica_groups=mesh['loop'=16,'narrow'=2] {'loop'}, dimensions={0}, use_global_device_ids=true | all-gather | bytes 557056 | tf_op jit(solution)/shard_map/all_gather | solution.py:37
  37.4 0.1 reshape.31
  37.5 0.7 add_rsqrt_fusion
  38.2 0.2 convert_reduce_fusion.2
  38.4 0.2 convert_reduce_fusion
  38.6 0.0 copy-done
  38.6 0.0 copy-done.2
  38.6 0.9 fusion.26
  39.4 1.7 %fusion.8 = f32[64,4096]{1,0:T(8,128)} fusion(bf16[256,4096]{1,0:T(8,128)(2,1)S(1)} %copy-done, f32[256]{0:T(256)S(1)} %get-tuple-element.20, f32[256,64]{0,1:T(8,128)S(1)} %get-tuple-element.4, f32[256]{0:T(256)S(1)} %get-tuple-element.3, f32[256]{0:T(256)S(1)} %get-tuple-element.21, s32[256]{0:T(256)S(1)} %copy-done.2), kind=kOutput, calls=%fused_computation.11 | convolution fusion | flops 137461760 | bytes 3215360 | tf_op jit(solution)/shard_map/dot_general | solution.py:57
  41.1 0.0 all-reduce.3.cloned.1.call-update
  41.1 0.9 fusion.3
  42.1 0.0 copy-start.3
  42.1 0.0 copy-start.1
  42.1 2.5 %fusion.6 = bf16[256,4096]{1,0:T(8,128)(2,1)} fusion(f32[256,4096]{1,0:T(8,128)S(1)} %get-tuple-element.15, bf16[256,4096]{1,0:T(8,128)(2,1)S(1)} %copy-done, f32[256]{0:T(256)S(1)} %get-tuple-element.14, f32[256]{0:T(256)S(1)} %get-tuple-element.20), kind=kLoop, calls=%fused_computation.8 | loop fusion | flops 6291456 | bytes 8390656 | tf_op jit(solution)/shard_map/convert_element_type | solution.py:31
  44.6 0.0 copy-done.3
  44.6 0.6 dynamic-slice
  45.8 0.6 log_subtract_fusion
  46.4 86.0 %all-reduce.3.cloned.1.call-done = f32[64,4096]{1,0:T(8,128)} async-done(((f32[64,4096]{1,0:T(8,128)}), f32[64,4096]{1,0:T(8,128)}) %all-reduce.3.cloned.1.call-update) | async-done | bytes 1048592
  132.4 0.9 dynamic-slice_bitcast_fusion
  133.3 4.9 %all-gather.2 = f32[2,4,4096]{2,1,0:T(4,128)S(1)} all-gather(f32[1,4,4096]{2,1,0:T(4,128)S(1)} %dynamic-slice_bitcast_fusion), channel_id=2, replica_groups=mesh['loop'=16,'narrow'=2] {'narrow'}, dimensions={0}, use_global_device_ids=true | all-gather | bytes 196608 | tf_op jit(solution)/shard_map/all_gather | solution.py:62
  138.3 0.0 copy-done.1
  138.3 0.2 fusion.18
  138.5 0.7 fusion.21
  (3 shorter events, 0.0 us)
Async XLA Ops:
  7.2 31.4 %copy-start = (bf16[256,4096]{1,0:T(8,128)(2,1)S(1)}, bf16[256,4096]{1,0:T(8,128)(2,1)}, u32[]{:S(2)}) copy-start(bf16[256,4096]{1,0:T(8,128)(2,1)} %param.7) | copy-start | bytes 6291460
  7.2 31.4 %copy-start.2 = (s32[256]{0:T(256)S(1)}, s32[256]{0:T(256)}, u32[]{:S(2)}) copy-start(s32[256]{0:T(256)} %param.9) | copy-start | bytes 3076
  7.2 125.2 %all-reduce.3.cloned.1.call-start = ((), (), s32[]{:S(2)}) async-start(), calls=%async_computation | async-start | bytes 2097152
  42.1 2.5 %copy-start.3 = (u32[32]{0:T(128)S(1)}, u32[32]{0:T(128)}, u32[]{:S(2)}) copy-start(u32[32]{0:T(128)} %constant.15) | copy-start | bytes 388
  42.1 96.2 %copy-start.1 = (bf16[4,4096]{1,0:T(4,128)(2,1)S(1)}, bf16[4,4096]{1,0:T(4,128)(2,1)}, u32[]{:S(2)}) copy-start(bf16[4,4096]{1,0:T(4,128)(2,1)} %param.8) | copy-start | bytes 98308
Sparse Core Ops, SparseCore 0:
  41.3 91.0 all-reduce.2
